TPU v7x, 32 devices: a whole 2x2x4 slice. The times are simulated.
32 devices in a mesh: group: 2 (over y), row: 4 (over z), col: 4 (over x, core).
Axes of the slice: x: 2, y: 2, z: 4, core: 2. Of those that a mesh axis runs over, the one named last changes fastest.
Arguments:
- tokens: bfloat16 [256, 5120], P('row', ('group', 'col')), may hold values from -6 to 6
- cotangent: bfloat16 [256, 12800], P(('group', 'col'), 'row'), may hold values from -0.375 to 0.375
- master: float32 [12800, 5120], P('row', ('group', 'col')), may hold values from -0.078125 to 0.078125
- moment: float32 [12800, 5120], P('row', ('group', 'col')), may hold values from -6 to 6
- second: float32 [12800, 5120], P('row', ('group', 'col')), may hold values from 0.1 to 4
- prompts: bfloat16 [512, 5120], P(('group', 'col')), may hold values from -6 to 6
- up_weight: bfloat16 [12800, 5120], P('row'), may hold values from -0.078125 to 0.078125
- down_weight: bfloat16 [12800, 5120], P('row'), may hold values from -0.0546875 to 0.0546875
Outputs:
- master_new: float32 [12800, 5120], P('row', ('group', 'col'))
- moment_new: float32 [12800, 5120], P('row', ('group', 'col'))
- second_new: float32 [12800, 5120], P('row', ('group', 'col'))
- prefill: float32 [512, 5120], P(('group', 'col'), 'row')
All inputs are finite; a program needn't handle non-finite values.
Results may differ from a plain program's by a relative error of at most 0.0041.
Values may be sent and summed in bfloat16 or wider, within the bound.
No kernel may reach another device: no remote copies, remote signals or barrier semaphores. Data moves between devices by JAX's collectives and lax.ppermute only.
A program may use at most 192 MiB of HBM per device.

v0:
```python
import jax
import jax.numpy as jnp
from jax import lax
from jax.sharding import PartitionSpec as P

beta_first = 0.9
beta_second = 0.95
learn_rate = 0.002
weight_decay = 0.1
epsilon = 1e-08
first_bias = 1.0 - 0.9**10
second_bias = 1.0 - 0.95**10


def adam_update(gradient, master, moment, second):
    moment_new = beta_first * moment + (1.0 - beta_first) * gradient
    second_new = beta_second * second + (1.0 - beta_second) * gradient * gradient
    direction = moment_new / first_bias / (jnp.sqrt(second_new / second_bias) + epsilon)
    master_new = master - learn_rate * (direction + weight_decay * master)
    return (master_new, moment_new, second_new)


def shards(tokens, cotangent, master, moment, second, prompts, up_weight, down_weight):
    cotangent_all = lax.all_gather(cotangent, ("group", "col"), axis=0, tiled=True)
    window = cotangent_all
    gradient = jnp.einsum(
        "tf,td->fd",
        window,
        lax.all_gather(tokens, "row", axis=0, tiled=True),
        preferred_element_type=jnp.float32,
    )
    master_new, moment_new, second_new = adam_update(gradient, master, moment, second)
    refreshed = master_new.astype(jnp.bfloat16)
    prompt_cols = lax.all_to_all(prompts, ("group", "col"), split_axis=1, concat_axis=0, tiled=True)
    window = prompt_cols
    gate_pre = lax.psum_scatter(
        jnp.einsum("nd,fd->nf", window, refreshed, preferred_element_type=jnp.float32),
        ("group", "col"),
        scatter_dimension=0,
        tiled=True,
    )
    up_pre = jnp.einsum("nd,fd->nf", prompts, up_weight, preferred_element_type=jnp.float32)
    hidden = (jax.nn.silu(gate_pre) * up_pre).astype(jnp.bfloat16)
    window = down_weight
    prefill = lax.psum_scatter(
        jnp.einsum("fd,nf->dn", window, hidden, preferred_element_type=jnp.float32),
        "row",
        scatter_dimension=0,
        tiled=True,
    ).T
    return (master_new, moment_new, second_new, prefill)


def solution(mesh):
    in_specs = (
        P("row", ("group", "col")),
        P(("group", "col"), "row"),
        P("row", ("group", "col")),
        P("row", ("group", "col")),
        P("row", ("group", "col")),
        P(("group", "col"), None),
        P("row", None),
        P("row", None),
    )
    out_specs = (
        P("row", ("group", "col")),
        P("row", ("group", "col")),
        P("row", ("group", "col")),
        P(("group", "col"), "row"),
    )
    return jax.shard_map(shards, mesh=mesh, in_specs=in_specs, out_specs=out_specs, check_vma=False)
```

profile of v0, /device:TPU:0, one launch (start us, length us, event | category | flops | bytes accessed | tf_op | source)
XLA Modules:
  0.0 207.8 jit_solution(4149311158553563539)
XLA Ops:
  7.2 0.0 all-gather.2.cloned.1.call-start
  7.2 0.7 all-gather.2.cloned.1.call-update
  7.9 2.0 copy.21
  9.9 5.2 %all-to-all-start = ((bf16[64,8,640]{2,0,1:T(8,128)(2,1)}), bf16[64,8,640]{2,0,1:T(8,128)(2,1)S(1)}, u32[]{:S(2)}, u32[]{:S(2)}) async-start(bf16[64,8,640]{2,0,1:T(8,128)(2,1)} %bitcast.18), calls=%async_computation | async-start | bytes 1310720 | tf_op jit(solution)/shard_map/all_to_all | solution.py:34
  15.1 0.0 reduce-scatter.7.cloned.1.call-start
  15.2 14.8 %all_gather.7 = bf16[256,640]{1,0:T(8,128)(2,1)S(1)} all-gather(bf16[64,640]{1,0:T(8,128)(2,1)} %param.8), channel_id=1, replica_groups=mesh['group'=2,'row'=4,'col'=4] {'row'}, dimensions={0}, use_global_device_ids=true | all-gather | bytes 409600 | tf_op jit(solution)/shard_map/all_gather | solution.py:29
  30.0 11.3 %all-gather.2.cloned.1.call-done = bf16[256,3200]{1,0:T(8,128)(2,1)} async-done(((bf16[32,3200]{1,0:T(8,128)(2,1)}), bf16[256,3200]{1,0:T(8,128)(2,1)}) %all-gather.2.cloned.1.call-update) | async-done | bytes 1638416 | tf_op jit(solution)/shard_map/all_gather | solution.py:24
  41.3 21.8 %multiply_subtract_fusion = (f32[3200,640]{1,0:T(8,128)}, f32[3200,640]{1,0:T(8,128)}, f32[3200,640]{1,0:T(8,128)}) fusion(f32[3200,640]{1,0:T(8,128)} %param.10, f32[3200,640]{1,0:T(8,128)} %param.11, f32[3200,640]{1,0:T(8,128)} %param.12, bf16[256,3200]{1,0:T(8,128)(2,1)} %all-gather.2.cloned.1.call-done, bf16[256,640]{1,0:T(8,128)(2,1)S(1)} %all_gather.7), kind=kOutput, calls=%fused_computation.2 | convolution fusion | flops 1079296000 | bytes 51118080 | tf_op jit(solution)/shard_map/tf,td->fd/dot_general | solution.py:26
  63.1 0.0 all-to-all-done
  63.1 8.1 %convolution_bitcast_fusion = f32[512,3200]{0,1:T(8,128)} fusion(bf16[512,640]{1,0:T(8,128)(2,1)S(1)} %bitcast.20, f32[3200,640]{1,0:T(8,128)} %get-tuple-element.4), kind=kOutput, calls=%fused_computation.4 | convolution fusion | flops 2099200000 | bytes 15400960 | tf_op jit(solution)/shard_map/nd,fd->nf/dot_general | solution.py:37
  71.2 0.0 copy-start
  71.2 8.2 %copy.17 = f32[512,3200]{1,0:T(8,128)} copy(f32[512,3200]{0,1:T(8,128)} %convolution_bitcast_fusion) | data formatting | bytes 13107200
  79.4 0.0 reduce-scatter.7.cloned.1.call-update
  79.4 0.0 reduce-scatter.5.cloned.1.call-start
  79.5 63.1 %reduce-scatter.7.cloned.1.call-done = f32[64,3200]{1,0:T(8,128)} async-done(((f32[512,3200]{1,0:T(8,128)}), f32[64,3200]{1,0:T(8,128)}) %reduce-scatter.7.cloned.1.call-update) | async-done | bytes 819216 | tf_op jit(solution)/shard_map/reduce_scatter | solution.py:36
  142.6 0.0 copy-done
  142.6 27.1 %convolution_bitcast_fusion.1 = f32[5120,64]{0,1:T(8,128)} fusion(bf16[3200,5120]{1,0:T(8,128)(2,1)} %param.15, bf16[64,5120]{1,0:T(8,128)(2,1)S(1)} %copy-done, bf16[3200,5120]{1,0:T(8,128)(2,1)} %param.14, f32[64,3200]{1,0:T(8,128)} %reduce-scatter.7.cloned.1.call-done), kind=kOutput, calls=%fused_computation.5 | convolution fusion | flops 4195532800 | bytes 68321280 | tf_op jit(solution)/shard_map/fd,nf->dn/dot_general | solution.py:46
  169.7 0.0 reduce-scatter.5.cloned.1.call-update
  169.7 31.5 %reduce-scatter.5.cloned.1.call-done = f32[1280,64]{0,1:T(8,128)} async-done(((f32[5120,64]{0,1:T(8,128)}), f32[1280,64]{0,1:T(8,128)}) %reduce-scatter.5.cloned.1.call-update) | async-done | bytes 327696 | tf_op jit(solution)/shard_map/reduce_scatter | solution.py:45
Async XLA Ops:
  7.2 34.1 %all-gather.2.cloned.1.call-start = ((), (), s32[]{:S(2)}) async-start(), calls=%async_computation.3 | async-start | bytes 1843200 | tf_op jit(solution)/shard_map/all_gather | solution.py:24
  9.9 53.2 %all-to-all-start = ((bf16[64,8,640]{2,0,1:T(8,128)(2,1)}), bf16[64,8,640]{2,0,1:T(8,128)(2,1)S(1)}, u32[]{:S(2)}, u32[]{:S(2)}) async-start(bf16[64,8,640]{2,0,1:T(8,128)(2,1)} %bitcast.18), calls=%async_computation | async-start | bytes 1310720 | tf_op jit(solution)/shard_map/all_to_all | solution.py:34
  15.1 127.5 %reduce-scatter.7.cloned.1.call-start = ((), (), s32[]{:S(2)}) async-start(), calls=%async_computation.5 | async-start | bytes 7372800 | tf_op jit(solution)/shard_map/reduce_scatter | solution.py:36
  71.2 71.4 %copy-start = (bf16[64,5120]{1,0:T(8,128)(2,1)S(1)}, bf16[64,5120]{1,0:T(8,128)(2,1)}, u32[]{:S(2)}) copy-start(bf16[64,5120]{1,0:T(8,128)(2,1)} %param.13) | copy-start | bytes 1966084
  79.4 121.8 %reduce-scatter.5.cloned.1.call-start = ((), (), s32[]{:S(2)}) async-start(), calls=%async_computation.4 | async-start | bytes 1638400 | tf_op jit(solution)/shard_map/reduce_scatter | solution.py:45
Sparse Core Ops, SparseCore 0:
  9.9 31.4 all-gather.1
  79.5 63.0 reduce-scatter.6
  169.8 31.3 reduce-scatter.4
where the time goes:
time: 208 us
  waiting for transfers between devices  107 us (51%)
  matrix products  57 us (27%)
  blocking collectives  14.8 us (7%)
  between operations  13.7 us (7%)
  local copies, waits for them, and re-layouts  10.2 us (5%)
  starting transfers between devices  5.32 us (3%)
    reduce_scatter x1, waiting for transfers between devices, shards(): lax.psum_scatter(jnp.einsum('nd,fd->nf', window, refreshed, preferred_ele...  63.1 us
    reduce_scatter x1, waiting for transfers between devices, shards(): lax.psum_scatter(jnp.einsum('fd,nf->dn', window, hidden, preferred_elemen...  31.5 us
    dot_general x1, matrix products, shards(): jnp.einsum('fd,nf->dn', window, hidden, preferred_element_type=jnp.float32)  27.1 us
    dot_general x1, matrix products, shards(): jnp.einsum('tf,td->fd', window, lax.all_gather(tokens, 'row', axis=0, til...  21.8 us
    all_gather x1, blocking collectives, shards(): lax.all_gather(tokens, 'row', axis=0, tiled=True)  14.8 us
    all_gather x1, waiting for transfers between devices, shards(): lax.all_gather(cotangent, ('group', 'col'), axis=0, tiled=True)  11.3 us
    unnamed x3, local copies, waits for them, and re-layouts  8.2 us
    dot_general x1, matrix products, shards(): jnp.einsum('nd,fd->nf', window, refreshed, preferred_element_type=jnp.flo...  8.08 us
  transfers between devices with their start and end apart: 4, of which 3 were waited for; matrix products, arithmetic and copies ran while one was open for 11% of the time, Pallas kernels for 0%

commit v1 on v0

v1 whole, which is shorter than its diff:
```python
import functools

import jax
import jax.numpy as jnp
from jax import lax
from jax.experimental import pallas as pl
from jax.experimental.pallas import tpu as pltpu
from jax.sharding import PartitionSpec as P


beta_first = 0.9
beta_second = 0.95
learn_rate = 0.002
weight_decay = 0.1
epsilon = 1e-08
first_bias = 1.0 - 0.9**10
second_bias = 1.0 - 0.95**10


bf16 = jnp.bfloat16
f32 = jnp.float32
lanes = 128
tile_choice = (640, 512, 384, 256, 128)


def adam_update(gradient, master, moment, second):
    moment_new = beta_first * moment + (1.0 - beta_first) * gradient
    second_new = beta_second * second + (1.0 - beta_second) * gradient * gradient
    direction = moment_new / first_bias / (jnp.sqrt(second_new / second_bias) + epsilon)
    master_new = master - learn_rate * (direction + weight_decay * master)
    return (master_new, moment_new, second_new)


def adam_folded(gradient, master, moment, second):
    moment_new = beta_first * moment + (1.0 - beta_first) * gradient
    second_new = beta_second * second + ((1.0 - beta_second) * gradient) * gradient
    scaled = second_new * (1.0 / second_bias)
    root = scaled * lax.rsqrt(scaled) + epsilon
    master_new = (1.0 - learn_rate * weight_decay) * master - (learn_rate / first_bias) * moment_new / root
    return (master_new, moment_new, second_new)


def plain(tokens, cotangent, master, moment, second, prompts, up_weight, down_weight):
    cotangent_all = lax.all_gather(cotangent, ("group", "col"), axis=0, tiled=True)
    gradient = jnp.einsum(
        "tf,td->fd",
        cotangent_all,
        lax.all_gather(tokens, "row", axis=0, tiled=True),
        preferred_element_type=f32,
    )
    master_new, moment_new, second_new = adam_update(gradient, master, moment, second)
    refreshed = master_new.astype(bf16)
    prompt_cols = lax.all_to_all(prompts, ("group", "col"), split_axis=1, concat_axis=0, tiled=True)
    gate_pre = lax.psum_scatter(
        jnp.einsum("nd,fd->nf", prompt_cols, refreshed, preferred_element_type=f32),
        ("group", "col"),
        scatter_dimension=0,
        tiled=True,
    )
    up_pre = jnp.einsum("nd,fd->nf", prompts, up_weight, preferred_element_type=f32)
    hidden = (jax.nn.silu(gate_pre) * up_pre).astype(bf16)
    prefill = lax.psum_scatter(
        jnp.einsum("fd,nf->dn", down_weight, hidden, preferred_element_type=f32),
        "row",
        scatter_dimension=0,
        tiled=True,
    ).T
    return (master_new, moment_new, second_new, prefill)


def full(shape):
    return pl.BlockSpec(shape, lambda *a: (0,) * len(shape))


resident = pl.BlockSpec(memory_space=pltpu.VMEM)


def params(mebibytes):
    return pltpu.CompilerParams(vmem_limit_bytes=mebibytes << 20)


def prompt_tiles(where, own, other, tile, count, at):
    rows = own.shape[0]

    def kernel(where_ref, own_ref, other_ref, *tile_refs):
        core = where_ref[0]
        for j in range(count):
            cols = pl.ds(pl.multiple_of(where_ref[at + j] * tile, lanes), tile)
            for ref, side in ((own_ref, core), (other_ref, 1 - core)):
                to = pl.ds(pl.multiple_of(side * rows, rows), rows)
                tile_refs[j][to, :] = ref[:, cols]

    return pl.pallas_call(
        kernel,
        grid_spec=pltpu.PrefetchScalarGridSpec(
            num_scalar_prefetch=1, grid=(1,), in_specs=[resident] * 2, out_specs=[resident] * count
        ),
        out_shape=[jax.ShapeDtypeStruct((2 * rows, tile), bf16)] * count,
        compiler_params=params(8),
        name="prompt_tiles",
    )(where, own, other)


def up_product(where, own, other, up_weight, tile):
    rows, width = own.shape
    hidden = up_weight.shape[0]
    half = tile // 2

    def kernel(where_ref, own_ref, other_ref, w_ref, o_ref, held):
        @pl.when(pl.program_id(0) == 0)
        def _():
            core = where_ref[0]
            for ref, side in ((own_ref, core), (other_ref, 1 - core)):
                held[pl.ds(pl.multiple_of(side * rows, rows), rows), :] = ref[...]

        o_ref[...] = lax.dot_general(
            w_ref[...], held[...], (((1,), (1,)), ((), ())), preferred_element_type=f32
        )

    return pl.pallas_call(
        kernel,
        grid_spec=pltpu.PrefetchScalarGridSpec(
            num_scalar_prefetch=1,
            grid=(hidden // tile,),
            in_specs=[
                full((rows, width)),
                full((rows, width)),
                pl.BlockSpec((half, width), lambda i, w: (2 * i + w[0], 0)),
            ],
            out_specs=pl.BlockSpec((half, 2 * rows), lambda i, w: (i, 0)),
            scratch_shapes=[pltpu.VMEM((2 * rows, width), bf16)],
        ),
        out_shape=jax.ShapeDtypeStruct((hidden // 2, 2 * rows), f32),
        compiler_params=params(24),
        cost_estimate=pl.CostEstimate(
            flops=2 * hidden * rows * width, transcendentals=0, bytes_accessed=hidden * width
        ),
        name="up_product",
    )(where, own, other, up_weight)


def fetch(arrays):
    n = len(arrays)

    def kernel(*refs):
        copies = [pltpu.make_async_copy(refs[i], refs[n + i], refs[2 * n].at[i]) for i in range(n)]
        for copy in copies:
            copy.start()
        for copy in copies:
            copy.wait()

    return pl.pallas_call(
        kernel,
        in_specs=[pl.BlockSpec(memory_space=pl.ANY)] * n,
        out_specs=[resident] * n,
        out_shape=[jax.ShapeDtypeStruct(a.shape, a.dtype) for a in arrays],
        scratch_shapes=[pltpu.SemaphoreType.DMA((n,))],
        compiler_params=params(8),
        cost_estimate=pl.CostEstimate(
            flops=0, transcendentals=0, bytes_accessed=sum(a.size * a.dtype.itemsize for a in arrays)
        ),
        name="fetch",
    )(*arrays)


def refresh(where, pieces, token_pieces, prompt_cols, state, previous, tile, first, count):
    hidden, width = state[0].shape
    half = tile // 2
    n, q, z = len(pieces), len(prompt_cols), len(token_pieces)
    step = pieces[0].shape[0]
    rows = prompt_cols[0].shape[0]
    spread = token_pieces[0].shape[0]
    orders = 5

    def kernel(where_ref, *refs):
        piece_refs, refs = refs[:n], refs[n:]
        token_refs, refs = refs[:z], refs[z:]
        col_refs, refs = refs[:q], refs[q:]
        state_refs, refs = refs[:3], refs[3:]
        refs = refs[len(previous) :]
        new_refs, refs = refs[:3], refs[3:]
        send_ref, keep_ref, window, turned, held, token_ref = refs
        i, s = pl.program_id(0), pl.program_id(1)
        core = where_ref[0]

        @pl.when((i == 0) & (s == 0))
        def _():
            for j in range(q):
                turned[:, j * rows : (j + 1) * rows] = col_refs[j][...].T
            for m in range(z):
                to = pl.ds(pl.multiple_of(where_ref[orders + m] * spread, spread), spread)
                held[to, :] = token_refs[m][...]
            for j in range(n):
                source = pl.ds(pl.multiple_of(where_ref[orders + z + j] * step, step), step)
                token_ref[j * step : (j + 1) * step, :] = held[source, :]

        @pl.when(s == 0)
        def _():
            cols = pl.ds(pl.multiple_of((first + i) * tile, lanes), tile)
            window[...] = jnp.concatenate([ref[:, cols] for ref in piece_refs], axis=0).T

        side = jnp.where(s == 0, 1 - core, core)
        part = jnp.dot(
            window[pl.ds(pl.multiple_of(side * half, half), half), :],
            token_ref[...],
            preferred_element_type=f32,
        )
        at = pl.ds(pl.multiple_of((2 * (first + i) + side) * half, half), half)
        new = adam_folded(part, *[ref[at, :] for ref in state_refs])
        for ref, value in zip(new_refs, new):
            ref[...] = value
        product = jnp.dot(new[0].astype(bf16), turned[...], preferred_element_type=f32)
        to = pl.ds(pl.multiple_of(i * half, half), half)

        @pl.when(s == 0)
        def _():
            send_ref[to, :] = product.astype(send_ref.dtype)

        @pl.when(s == 1)
        def _():
            keep_ref[to, :] = product.astype(keep_ref.dtype)

    def at(i, s, w):
        return (2 * (first + i) + jnp.where(s == 0, 1 - w[0], w[0]), 0)

    block = pl.BlockSpec((half, width), at)
    out = [jax.ShapeDtypeStruct((hidden, width), f32)] * 3
    out += [jax.ShapeDtypeStruct((count * half, q * rows), t) for t in (bf16, f32)]
    return pl.pallas_call(
        kernel,
        grid_spec=pltpu.PrefetchScalarGridSpec(
            num_scalar_prefetch=1,
            grid=(count, 2),
            in_specs=[resident] * (n + z + q + 3) + [pl.BlockSpec(memory_space=pl.ANY)] * len(previous),
            out_specs=[block] * 3 + [resident] * 2,
            scratch_shapes=[
                pltpu.VMEM((tile, n * step), bf16),
                pltpu.VMEM((width, q * rows), bf16),
                pltpu.VMEM((n * step, width), bf16),
                pltpu.VMEM((n * step, width), bf16),
            ],
        ),
        out_shape=out,
        input_output_aliases={1 + n + z + q + 3 + m: m for m in range(len(previous))},
        compiler_params=params(16),
        cost_estimate=pl.CostEstimate(
            flops=2 * count * tile * width * (n * step + q * rows),
            transcendentals=count * tile * width,
            bytes_accessed=24 * count * tile * width,
        ),
        name="refresh",
    )(where, *pieces, *token_pieces, *prompt_cols, *state, *previous)


def join_cores(keep, received, rows):
    parts = []
    for j in range(keep.shape[1] // rows):
        cut = slice(j * rows, (j + 1) * rows)
        total = keep[:, cut] + received[:, cut].astype(f32)
        parts.append(total.astype(bf16) if j else total)
    return parts


def activate(own, received, up_pre):
    for value in received:
        own = own + value.astype(f32)
    return (jax.nn.silu(own) * up_pre).astype(bf16)


def down_product(where, own, other, down_weight, tile, cols, types, slots):
    hidden = down_weight.shape[0]
    half = tile // 2
    n = len(own)
    rows = own[0].shape[1]
    counts = [a.shape[0] // half for a in own]

    def kernel(where_ref, *refs):
        own_refs, other_refs, w_ref = refs[:n], refs[n : 2 * n], refs[2 * n]
        out_refs, (held, turned) = refs[2 * n + 1 : -2], refs[-2:]
        core = where_ref[0]
        i = pl.program_id(0)

        @pl.when(i == 0)
        def _():
            base = 0
            for c in range(n):
                for t in range(counts[c]):
                    for ref, side in ((own_refs[c], core), (other_refs[c], 1 - core)):
                        at = pl.multiple_of(base + side * half, half)
                        held[pl.ds(at, half), :] = ref[t * half : (t + 1) * half, :]
                    base += tile
            turned[...] = held[...].T

        product = jnp.dot(turned[...], w_ref[...], preferred_element_type=f32)
        for j in range(len(types)):

            @pl.when(i == j)
            def _():
                out_refs[j][...] = product.astype(types[j])

    def at(i, w):
        return (0, 2 * w[slots + i] + w[0])

    return pl.pallas_call(
        kernel,
        grid_spec=pltpu.PrefetchScalarGridSpec(
            num_scalar_prefetch=1,
            grid=(len(types),),
            in_specs=[full(a.shape) for a in own + other] + [pl.BlockSpec((hidden, cols), at)],
            out_specs=[full((rows, cols))] * len(types),
            scratch_shapes=[pltpu.VMEM((hidden, rows), bf16), pltpu.VMEM((rows, hidden), bf16)],
        ),
        out_shape=[jax.ShapeDtypeStruct((rows, cols), t) for t in types],
        compiler_params=params(24),
        cost_estimate=pl.CostEstimate(
            flops=2 * hidden * rows * cols * len(types),
            transcendentals=0,
            bytes_accessed=2 * hidden * cols * len(types),
        ),
        name="down_product",
    )(where, *own, *other, down_weight)


def staged(sizes, tile, tokens, cotangent, master, moment, second, prompts, up_weight, down_weight):
    groups, rows, cols = sizes
    chips = cols // 2
    plane = ("group", "col")
    offsets = [(g, x) for g in range(groups) for x in range(chips)]
    offsets = [o for o in offsets if o != (0, 0)]

    def move(value, dg, dx, dk=0):
        pairs = []
        for g in range(groups):
            for c in range(cols):
                x, k = c // 2, c % 2
                to = ((x + dx) % chips) * 2 + (k + dk) % 2
                pairs.append((g * cols + c, ((g + dg) % groups) * cols + to))
        return lax.ppermute(value, plane, pairs)

    def swap(value):
        return move(value, 0, 0, 1)

    def row_swap(value, bit):
        return lax.ppermute(value, "row", [(i, i ^ bit) for i in range(rows)])

    group, row, col = (lax.axis_index(a) for a in ("group", "row", "col"))
    chip, core = col // 2, col % 2

    def place(dg, dx, k):
        return ((group + dg) % groups) * cols + ((chip + dx) % chips) * 2 + k

    relative = [0]
    bit = rows // 2
    while bit:
        relative += [m ^ bit for m in relative]
        bit //= 2
    index = [core, row ^ 3, row ^ 1, row ^ 2, row] + [row ^ m for m in relative]
    for k in (core, 1 - core):
        index += [place(0, 0, k)] + [place(-o[0], -o[1], k) for o in offsets]
    tiles_at = len(index)
    index += [place(0, 0, core)] + [place(*o, core) for o in offsets]
    where = jnp.stack(index)

    other_prompts = swap(prompts)
    tiles = prompt_tiles(
        where, prompts, other_prompts, master.shape[1], 1 + len(offsets), tiles_at
    )
    tiles, cotangent, tokens = lax.optimization_barrier((tiles, cotangent, tokens))
    prompt_cols, own = [tiles[0]], [cotangent]
    for o, tile_of in zip(offsets, tiles[1:]):
        own.append(move(cotangent, *o))
        prompt_cols.append(move(tile_of, *o))

    token_pieces = [tokens]
    bit = rows // 2
    while bit:
        both = jnp.concatenate(token_pieces, 0)
        token_pieces = [both, row_swap(both, bit)]
        bit //= 2
    spread = tokens.shape[0]
    token_pieces = [t[m : m + spread] for t in token_pieces for m in range(0, t.shape[0], spread)]

    state = fetch((master, moment, second))
    pieces = own + [swap(p) for p in own]

    total_tiles = master.shape[0] // tile
    head = (total_tiles + 1) // 2
    new = ()
    gates = []
    for first, count in ((0, head), (head, total_tiles - head)):
        *new, send, keep = refresh(
            where, pieces, token_pieces, prompt_cols, state, new, tile, first, count
        )
        mine, *away = join_cores(keep, swap(send), prompt_cols[0].shape[0])
        mine, away, new = lax.optimization_barrier((mine, away, new))
        back = [move(a, -o[0], -o[1]) for a, o in zip(away, offsets)]
        gates.append((mine, back))
    up_pre = up_product(where, prompts, other_prompts, up_weight, tile)
    acts = []
    at = 0
    for mine, back in gates:
        acts.append(activate(mine, back, up_pre[at : at + mine.shape[0]]))
        at += mine.shape[0]
    others = [swap(a) for a in acts]

    out_cols = down_weight.shape[1] // rows // 2
    far_pair, across = down_product(where, acts, others, down_weight, tile, out_cols, (bf16, bf16), 1)
    far, mine = down_product(where, acts, others, down_weight, tile, out_cols, (f32, f32), 3)
    from_pair = row_swap(far_pair, 1)
    from_near = row_swap(across, 1)
    from_far = row_swap((far + from_pair.astype(f32)).astype(bf16), 2)
    total = mine + from_near.astype(f32) + from_far.astype(f32)
    half = total.shape[0] // 2
    stay = lax.dynamic_slice_in_dim(total, core * half, half, 0)
    leave = swap(lax.dynamic_slice_in_dim(total, (1 - core) * half, half, 0))
    prefill = jnp.where(
        core == 0, jnp.concatenate([stay, leave], 1), jnp.concatenate([leave, stay], 1)
    )
    return (*new, prefill)


def shards(sizes, *arrays):
    tokens, cotangent, master, _, _, prompts, _, down_weight = arrays
    groups, rows, cols = sizes
    hidden, width = master.shape
    tiles = [t for t in tile_choice if hidden % t == 0 and hidden // t > 1 and t % 32 == 0]
    fits = (
        tiles
        and rows == 4
        and cols % 2 == 0
        and groups * cols > 2
        and width % lanes == 0
        and prompts.shape[0] * 2 == lanes
        and cotangent.shape[0] % 16 == 0
        and tokens.shape[0] % 16 == 0
        and down_weight.shape[1] % (2 * rows * lanes) == 0
    )
    if not fits:
        return plain(*arrays)
    return staged(sizes, tiles[0], *arrays)


def solution(mesh):
    in_specs = (
        P("row", ("group", "col")),
        P(("group", "col"), "row"),
        P("row", ("group", "col")),
        P("row", ("group", "col")),
        P("row", ("group", "col")),
        P(("group", "col"), None),
        P("row", None),
        P("row", None),
    )
    out_specs = (
        P("row", ("group", "col")),
        P("row", ("group", "col")),
        P("row", ("group", "col")),
        P(("group", "col"), "row"),
    )
    sizes = tuple(mesh.shape[a] for a in ("group", "row", "col"))
    return jax.shard_map(
        functools.partial(shards, sizes), mesh=mesh, in_specs=in_specs, out_specs=out_specs, check_vma=False
    )
```

time: 208 us -> 114 us (0.55)
  waiting for transfers between devices: 107 us -> 32.3 us
  matrix products: 57 us -> 0 us
  Pallas kernels: 0 us -> 40.9 us
  starting transfers between devices: 5.32 us -> 28.8 us
  blocking collectives: 14.8 us -> 0 us
  between operations: 13.7 us -> 0.84 us
  other arithmetic: 0 us -> 2.53 us
  local copies, waits for them, and re-layouts: 10.2 us -> 7.89 us
    reduce_scatter x2 -> x0, waiting for transfers between devices: 94.6 us -> none  [the longest x1 63.1 us: shards(): lax.psum_scatter(jnp.einsum('nd,fd->nf', window, refreshed, preferred_ele...]
    dot_general x3 -> x0, matrix products: 57 us -> none  [the longest x1 27.1 us: shards(): jnp.einsum('fd,nf->dn', window, hidden, preferred_element_type=jnp.float32)]
    pallas_call x0 -> x7, Pallas kernels: none -> 40.9 us  [the longest x2 16.4 us: refresh(): pl.pallas_call(kernel, grid_spec=pltpu.PrefetchScalarGridSpec(num_scalar_...]
    ppermute x0 -> x27, waiting for transfers between devices: none -> 32.3 us  [the longest x22 24.7 us: move(): return lax.ppermute(value, plane, pairs)]
    ppermute x0 -> x27, starting transfers between devices: none -> 28.8 us  [the longest x22 18.2 us: move(): return lax.ppermute(value, plane, pairs)]
    all_gather x1 -> x0, blocking collectives: 14.8 us -> none  [shards(): lax.all_gather(tokens, 'row', axis=0, tiled=True)]
    all_gather x1 -> x0, waiting for transfers between devices: 11.3 us -> none  [shards(): lax.all_gather(cotangent, ('group', 'col'), axis=0, tiled=True)]
    all_to_all x1 -> x0, starting transfers between devices: 5.2 us -> none  [shards(): lax.all_to_all(prompts, ('group', 'col'), split_axis=1, concat_axis=0, ti...]
  transfers between devices with their start and end apart: 4 -> 27, of which waited for: 3 -> 11; matrix products, arithmetic and copies ran while one was open for 11% -> 1% of each run, Pallas kernels for 0% -> 17%
where the time goes in v1:
time: 114 us; the launch traced here: 113 us
  Pallas kernels  40.9 us (36%)
  waiting for transfers between devices  32.3 us (28%)
  starting transfers between devices  28.8 us (25%)
  local copies, waits for them, and re-layouts  7.89 us (7%)
  other arithmetic  2.53 us (2%)
    ppermute x22, waiting for transfers between devices, move(): return lax.ppermute(value, plane, pairs)  24.7 us
    ppermute x22, starting transfers between devices, move(): return lax.ppermute(value, plane, pairs)  18.2 us
    pallas_call x2, Pallas kernels, refresh(): pl.pallas_call(kernel, grid_spec=pltpu.PrefetchScalarGridSpec(num_scalar_...  16.4 us
    ppermute x5, starting transfers between devices, row_swap(): return lax.ppermute(value, 'row', [(i, i ^ bit) for i in range(rows)])  10.6 us
    pallas_call x2, Pallas kernels, down_product(): pl.pallas_call(kernel, grid_spec=pltpu.PrefetchScalarGridSpec(num_scalar_...  9.68 us
    pallas_call x1, Pallas kernels, up_product(): pl.pallas_call(kernel, grid_spec=pltpu.PrefetchScalarGridSpec(num_scalar_...  9.53 us
    unnamed x12, local copies, waits for them, and re-layouts  7.75 us
    ppermute x5, waiting for transfers between devices, row_swap(): return lax.ppermute(value, 'row', [(i, i ^ bit) for i in range(rows)])  7.52 us
  transfers between devices with their start and end apart: 27, of which 11 were waited for; matrix products, arithmetic and copies ran while one was open for 1% of the time, Pallas kernels for 17%

profile of v1, /device:TPU:0, one launch (start us, length us, event | category | flops | bytes accessed | tf_op | source)
XLA Modules:
  0.0 113.2 jit_solution(17689114942390387948)
XLA Ops:
  1.3 1.8 %collective-permute-done.other_ref = bf16[64,5120]{1,0:T(8,128)(2,1)S(1)} collective-permute-done((bf16[64,5120]{1,0:T(8,128)(2,1)}, bf16[64,5120]{1,0:T(8,128)(2,1)S(1)}, u32[]{:S(2)}, u32[]{:S(2)}) %collective-permute-start) | collective-permute-done | bytes 655392 | tf_op jit(solution)/shard_map/ppermute | solution.py:338
  4.8 4.0 %collective-permute-start.8 = (bf16[64,640]{1,0:T(8,128)(2,1)}, bf16[64,640]{1,0:T(8,128)(2,1)S(1)}, u32[]{:S(2)}, u32[]{:S(2)}) collective-permute-start(bf16[64,640]{1,0:T(8,128)(2,1)} %refs_8_.1), channel_id=1, source_target_pairs={{0,8},{4,12},{8,0},{12,4},{1,9},{5,13},{9,1},{13,5},{2,10},{6,14},... | collective-permute-start | bytes 245768 | tf_op jit(solution)/shard_map/ppermute | solution.py:344
  10.9 1.5 %collective-permute-start.2 = (bf16[32,3200]{1,0:T(8,128)(2,1)}, bf16[32,3200]{1,0:T(8,128)(2,1)S(1)}, u32[]{:S(2)}, u32[]{:S(2)}) collective-permute-start(bf16[32,3200]{1,0:T(8,128)(2,1)} %refs_0_.3), channel_id=1, source_target_pairs={{0,16},{1,17},{2,18},{3,19},{16,0},{17,1},{18,2},{19,3},{4,20},{5,... | collective-permute-start | bytes 614408 | tf_op jit(solution)/shard_map/ppermute | solution.py:338
  13.8 1.5 %collective-permute-start.11 = (bf16[128,640]{1,0:T(8,128)(2,1)S(1)}, bf16[128,640]{1,0:T(8,128)(2,1)S(1)}, u32[]{:S(2)}, u32[]{:S(2)}) collective-permute-start(bf16[128,640]{1,0:T(8,128)(2,1)S(1)} %get-tuple-element.53), channel_id=1, source_target_pairs={{0,16},{1,17},{2,18},{3,19},{16,0},{17,1},{18,2},{19,3},{4,20},{5,... | collective-permute-start | bytes 491528 | tf_op jit(solution)/shard_map/ppermute | solution.py:338
  16.3 1.6 %collective-permute-start.9 = (bf16[128,640]{1,0:T(8,128)(2,1)S(1)}, bf16[128,640]{1,0:T(8,128)(2,1)S(1)}, u32[]{:S(2)}, u32[]{:S(2)}) collective-permute-start(bf16[128,640]{1,0:T(8,128)(2,1)S(1)} %pad_maximum_fusion), channel_id=1, source_target_pairs={{0,4},{4,0},{8,12},{12,8},{1,5},{5,1},{9,13},{13,9},{2,6},{6,2},{1... | collective-permute-start | bytes 491528 | tf_op jit(solution)/shard_map/ppermute | solution.py:344
  18.0 3.3 %copy-done = f32[3200,640]{1,0:T(8,128)S(1)} copy-done((f32[3200,640]{1,0:T(8,128)S(1)}, f32[3200,640]{1,0:T(8,128)}, u32[]{:S(2)}) %copy-start) | copy-done | bytes 8192024
  21.3 3.3 %copy-done.1 = f32[3200,640]{1,0:T(8,128)S(1)} copy-done((f32[3200,640]{1,0:T(8,128)S(1)}, f32[3200,640]{1,0:T(8,128)}, u32[]{:S(2)}) %copy-start.1) | copy-done | bytes 8192024
  24.6 4.6 %fetch.1 = (f32[3200,640]{1,0:T(8,128)S(1)}, f32[3200,640]{1,0:T(8,128)S(1)}, f32[3200,640]{1,0:T(8,128)S(1)}) custom-call(f32[3200,640]{1,0:T(8,128)S(1)} %copy-done, f32[3200,640]{1,0:T(8,128)S(1)} %copy-done.1, f32[3200,640]{1,0:T(8,128)} %refs_2_.1), custom_call_target="tpu_custom_call" | custom-call | bytes 24576000 | tf_op jit(solution)/shard_map/fetch/pallas_call | solution.py:152
  29.4 2.0 %collective-permute-start.12 = (bf16[128,640]{1,0:T(8,128)(2,1)S(1)}, bf16[128,640]{1,0:T(8,128)(2,1)S(1)}, u32[]{:S(2)}, u32[]{:S(2)}) collective-permute-start(bf16[128,640]{1,0:T(8,128)(2,1)S(1)} %get-tuple-element.54), channel_id=1, source_target_pairs={{0,18},{1,19},{2,16},{3,17},{16,2},{17,3},{18,0},{19,1},{4,22},{5,... | collective-permute-start | bytes 491528 | tf_op jit(solution)/shard_map/ppermute | solution.py:338
  32.1 4.8 %collective-permute-done.12.refs_15_ = bf16[128,640]{1,0:T(8,128)(2,1)S(1)} collective-permute-done((bf16[128,640]{1,0:T(8,128)(2,1)S(1)}, bf16[128,640]{1,0:T(8,128)(2,1)S(1)}, u32[]{:S(2)}, u32[]{:S(2)}) %collective-permute-start.12) | collective-permute-done | bytes 163872 | tf_op jit(solution)/shard_map/ppermute | solution.py:338
  36.9 9.5 %refresh.2 = (f32[3200,640]{1,0:T(8,128)}, f32[3200,640]{1,0:T(8,128)}, f32[3200,640]{1,0:T(8,128)}, bf16[960,512]{1,0:T(8,128)(2,1)S(1)}, f32[960,512]{1,0:T(8,128)S(1)}) custom-call(s32[21]{0:T(128)S(1)} %stack.72.where_ref, bf16[32,3200]{1,0:T(8,128)(2,1)S(1)} %copy-done.4, bf16[32,3200]{1,0:T(8,128)(2,1)S(1)} %collective-permute-done.1.refs_1_, ...), custom_call_target="tpu_custom_call" | custom-call | flops 1887436800 | bytes 29491200 | tf_op jit(solution)/shard_map/refresh/pallas_call | solution.py:229
  46.4 2.6 %collective-permute-done.13 = bf16[960,512]{1,0:T(8,128)(2,1)S(1)} collective-permute-done((bf16[960,512]{1,0:T(8,128)(2,1)S(1)}, bf16[960,512]{1,0:T(8,128)(2,1)S(1)}, u32[]{:S(2)}, u32[]{:S(2)}) %collective-permute-start.13) | collective-permute-done | bytes 983072 | tf_op jit(solution)/shard_map/ppermute | solution.py:338
  49.2 7.0 %refresh.3 = (f32[3200,640]{1,0:T(8,128)}, f32[3200,640]{1,0:T(8,128)}, f32[3200,640]{1,0:T(8,128)}, bf16[640,512]{1,0:T(8,128)(2,1)S(1)}, f32[640,512]{1,0:T(8,128)S(1)}) custom-call(s32[21]{0:T(128)S(1)} %stack.72.where_ref, bf16[32,3200]{1,0:T(8,128)(2,1)S(1)} %copy-done.4, ...), custom_call_target="tpu_custom_call", output_to_operand_aliasing={{0}: (20, {}), {1}: (21, {}), {2}: (22, {})} | custom-call | flops 1258291200 | bytes 19660800 | tf_op jit(solution)/shard_map/refresh/pallas_call | solution.py:229
  56.3 9.5 %up_product.1 = f32[1600,128]{1,0:T(8,128)S(1)} custom-call(s32[21]{0:T(128)S(1)} %stack.72.where_ref, bf16[64,5120]{1,0:T(8,128)(2,1)S(1)} %copy-done.3, bf16[64,5120]{1,0:T(8,128)(2,1)S(1)} %collective-permute-done.other_ref, bf16[3200,5120]{1,0:T(8,128)(2,1)} %w_ref.1), custom_call_target="tpu_custom_call" | custom-call | flops 2097152000 | bytes 16384000 | tf_op jit(solution)/shard_map/up_product/pallas_call | solution.py:120
  66.9 1.5 %collective-permute-start.16 = (bf16[960,128]{1,0:T(8,128)(2,1)S(1)}, bf16[960,128]{1,0:T(8,128)(2,1)S(1)}, u32[]{:S(2)}, u32[]{:S(2)}) collective-permute-start(bf16[960,128]{1,0:T(8,128)(2,1)S(1)} %get-tuple-element.76), channel_id=1, source_target_pairs={{0,16},{1,17},{2,18},{3,19},{16,0},{17,1},{18,2},{19,3},{4,20},{5,... | collective-permute-start | bytes 737288 | tf_op jit(solution)/shard_map/ppermute | solution.py:338
  72.1 2.6 %collective-permute-done.15 = bf16[960,128]{1,0:T(8,128)(2,1)S(1)} collective-permute-done((bf16[960,128]{1,0:T(8,128)(2,1)S(1)}, bf16[960,128]{1,0:T(8,128)(2,1)S(1)}, u32[]{:S(2)}, u32[]{:S(2)}) %collective-permute-start.15) | collective-permute-done | bytes 245792 | tf_op jit(solution)/shard_map/ppermute | solution.py:338
  74.7 1.9 %collective-permute-start.20 = (bf16[640,128]{1,0:T(8,128)(2,1)S(1)}, bf16[640,128]{1,0:T(8,128)(2,1)S(1)}, u32[]{:S(2)}, u32[]{:S(2)}) collective-permute-start(bf16[640,128]{1,0:T(8,128)(2,1)S(1)} %get-tuple-element.81), channel_id=1, source_target_pairs={{0,18},{1,19},{2,16},{3,17},{16,2},{17,3},{18,0},{19,1},{4,22},{5,... | collective-permute-start | bytes 491528 | tf_op jit(solution)/shard_map/ppermute | solution.py:338
  76.7 4.3 %collective-permute-done.16 = bf16[960,128]{1,0:T(8,128)(2,1)S(1)} collective-permute-done((bf16[960,128]{1,0:T(8,128)(2,1)S(1)}, bf16[960,128]{1,0:T(8,128)(2,1)S(1)}, u32[]{:S(2)}, u32[]{:S(2)}) %collective-permute-start.16) | collective-permute-done | bytes 245792 | tf_op jit(solution)/shard_map/ppermute | solution.py:338
  81.3 2.2 %collective-permute-done.18 = bf16[640,128]{1,0:T(8,128)(2,1)S(1)} collective-permute-done((bf16[640,128]{1,0:T(8,128)(2,1)S(1)}, bf16[640,128]{1,0:T(8,128)(2,1)S(1)}, u32[]{:S(2)}, u32[]{:S(2)}) %collective-permute-start.18) | collective-permute-done | bytes 163872 | tf_op jit(solution)/shard_map/ppermute | solution.py:338
  83.5 3.6 %collective-permute-done.19 = bf16[640,128]{1,0:T(8,128)(2,1)S(1)} collective-permute-done((bf16[640,128]{1,0:T(8,128)(2,1)S(1)}, bf16[640,128]{1,0:T(8,128)(2,1)S(1)}, u32[]{:S(2)}, u32[]{:S(2)}) %collective-permute-start.19) | collective-permute-done | bytes 163872 | tf_op jit(solution)/shard_map/ppermute | solution.py:338
  88.7 4.8 %down_product.3 = (bf16[128,640]{1,0:T(8,128)(2,1)S(1)}, bf16[128,640]{1,0:T(8,128)(2,1)S(1)}) custom-call(s32[21]{0:T(128)S(1)} %stack.72.where_ref, bf16[960,128]{1,0:T(8,128)(2,1)S(1)} %fusion.refs_0_, bf16[640,128]{1,0:T(8,128)(2,1)S(1)} %fusion.1.refs_1_, bf16[960,128]{1,0:T(8,128)(2,1)S(1)} %collective-permute-done.21.refs_2_, ...), custom_call_target="tpu_custom_call" | custom-call | flops 1048576000 | bytes 8192000 | tf_op jit(solution)/shard_map/down_product/pallas_call | solution.py:304
  95.7 4.8 %down_product.2 = (f32[128,640]{1,0:T(8,128)S(1)}, f32[128,640]{1,0:T(8,128)S(1)}) custom-call(s32[21]{0:T(128)S(1)} %stack.72.where_ref, bf16[960,128]{1,0:T(8,128)(2,1)S(1)} %fusion.refs_0_, bf16[640,128]{1,0:T(8,128)(2,1)S(1)} %fusion.1.refs_1_, bf16[960,128]{1,0:T(8,128)(2,1)S(1)} %collective-permute-done.21.refs_2_, ...), custom_call_target="tpu_custom_call" | custom-call | flops 1048576000 | bytes 8192000 | tf_op jit(solution)/shard_map/down_product/pallas_call | solution.py:304
  100.8 2.8 %collective-permute-start.25 = (bf16[128,640]{1,0:T(8,128)(2,1)S(1)}, bf16[128,640]{1,0:T(8,128)(2,1)S(1)}, u32[]{:S(2)}, u32[]{:S(2)}) collective-permute-start(bf16[128,640]{1,0:T(8,128)(2,1)S(1)} %add_convert_fusion.3), channel_id=1, source_target_pairs={{0,8},{4,12},{8,0},{12,4},{1,9},{5,13},{9,1},{13,5},{2,10},{6,14},... | collective-permute-start | bytes 491528 | tf_op jit(solution)/shard_map/ppermute | solution.py:344
  103.6 7.3 %collective-permute-done.25 = bf16[128,640]{1,0:T(8,128)(2,1)S(1)} collective-permute-done((bf16[128,640]{1,0:T(8,128)(2,1)S(1)}, bf16[128,640]{1,0:T(8,128)(2,1)S(1)}, u32[]{:S(2)}, u32[]{:S(2)}) %collective-permute-start.25) | collective-permute-done | bytes 163872 | tf_op jit(solution)/shard_map/ppermute | solution.py:344
  (60 shorter events, 19.2 us)
Async XLA Ops:
  4.8 9.0 %collective-permute-start.8 = (bf16[64,640]{1,0:T(8,128)(2,1)}, bf16[64,640]{1,0:T(8,128)(2,1)S(1)}, u32[]{:S(2)}, u32[]{:S(2)}) collective-permute-start(bf16[64,640]{1,0:T(8,128)(2,1)} %refs_8_.1), channel_id=1, source_target_pairs={{0,8},{4,12},{8,0},{12,4},{1,9},{5,13},{9,1},{13,5},{2,10},{6,14},... | collective-permute-start | bytes 245768 | tf_op jit(solution)/shard_map/ppermute | solution.py:344
  8.8 7.5 %collective-permute-start.10 = (bf16[128,640]{1,0:T(8,128)(2,1)S(1)}, bf16[128,640]{1,0:T(8,128)(2,1)S(1)}, u32[]{:S(2)}, u32[]{:S(2)}) collective-permute-start(bf16[128,640]{1,0:T(8,128)(2,1)S(1)} %get-tuple-element.52), channel_id=1, source_target_pairs={{0,2},{1,3},{2,0},{3,1},{16,18},{17,19},{18,16},{19,17},{4,6},{5,7... | collective-permute-start | bytes 491528 | tf_op jit(solution)/shard_map/ppermute | solution.py:338
  10.3 19.0 %collective-permute-start.1 = (bf16[32,3200]{1,0:T(8,128)(2,1)}, bf16[32,3200]{1,0:T(8,128)(2,1)S(1)}, u32[]{:S(2)}, u32[]{:S(2)}) collective-permute-start(bf16[32,3200]{1,0:T(8,128)(2,1)} %refs_0_.3), channel_id=1, source_target_pairs={{0,2},{1,3},{2,0},{3,1},{16,18},{17,19},{18,16},{19,17},{4,6},{5,7... | collective-permute-start | bytes 614408 | tf_op jit(solution)/shard_map/ppermute | solution.py:338
  10.9 20.5 %collective-permute-start.2 = (bf16[32,3200]{1,0:T(8,128)(2,1)}, bf16[32,3200]{1,0:T(8,128)(2,1)S(1)}, u32[]{:S(2)}, u32[]{:S(2)}) collective-permute-start(bf16[32,3200]{1,0:T(8,128)(2,1)} %refs_0_.3), channel_id=1, source_target_pairs={{0,16},{1,17},{2,18},{3,19},{16,0},{17,1},{18,2},{19,3},{4,20},{5,... | collective-permute-start | bytes 614408 | tf_op jit(solution)/shard_map/ppermute | solution.py:338
  12.4 19.2 %collective-permute-start.3 = (bf16[32,3200]{1,0:T(8,128)(2,1)}, bf16[32,3200]{1,0:T(8,128)(2,1)S(1)}, u32[]{:S(2)}, u32[]{:S(2)}) collective-permute-start(bf16[32,3200]{1,0:T(8,128)(2,1)} %refs_0_.3), channel_id=1, source_target_pairs={{0,18},{1,19},{2,16},{3,17},{16,2},{17,3},{18,0},{19,1},{4,22},{5,... | collective-permute-start | bytes 614408 | tf_op jit(solution)/shard_map/ppermute | solution.py:338
  13.8 15.4 %collective-permute-start.11 = (bf16[128,640]{1,0:T(8,128)(2,1)S(1)}, bf16[128,640]{1,0:T(8,128)(2,1)S(1)}, u32[]{:S(2)}, u32[]{:S(2)}) collective-permute-start(bf16[128,640]{1,0:T(8,128)(2,1)S(1)} %get-tuple-element.53), channel_id=1, source_target_pairs={{0,16},{1,17},{2,18},{3,19},{16,0},{17,1},{18,2},{19,3},{4,20},{5,... | collective-permute-start | bytes 491528 | tf_op jit(solution)/shard_map/ppermute | solution.py:338
  16.3 15.6 %collective-permute-start.9 = (bf16[128,640]{1,0:T(8,128)(2,1)S(1)}, bf16[128,640]{1,0:T(8,128)(2,1)S(1)}, u32[]{:S(2)}, u32[]{:S(2)}) collective-permute-start(bf16[128,640]{1,0:T(8,128)(2,1)S(1)} %pad_maximum_fusion), channel_id=1, source_target_pairs={{0,4},{4,0},{8,12},{12,8},{1,5},{5,1},{9,13},{13,9},{2,6},{6,2},{1... | collective-permute-start | bytes 491528 | tf_op jit(solution)/shard_map/ppermute | solution.py:344
  29.3 7.6 %collective-permute-start.4 = (bf16[32,3200]{1,0:T(8,128)(2,1)S(1)}, bf16[32,3200]{1,0:T(8,128)(2,1)S(1)}, u32[]{:S(2)}, u32[]{:S(2)}) collective-permute-start(bf16[32,3200]{1,0:T(8,128)(2,1)S(1)} %copy-done.4), channel_id=1, source_target_pairs={{0,1},{1,0},{2,3},{3,2},{16,17},{17,16},{18,19},{19,18},{4,5},{5,4... | collective-permute-start | bytes 614408 | tf_op jit(solution)/shard_map/ppermute | solution.py:338
  29.4 7.5 %collective-permute-start.12 = (bf16[128,640]{1,0:T(8,128)(2,1)S(1)}, bf16[128,640]{1,0:T(8,128)(2,1)S(1)}, u32[]{:S(2)}, u32[]{:S(2)}) collective-permute-start(bf16[128,640]{1,0:T(8,128)(2,1)S(1)} %get-tuple-element.54), channel_id=1, source_target_pairs={{0,18},{1,19},{2,16},{3,17},{16,2},{17,3},{18,0},{19,1},{4,22},{5,... | collective-permute-start | bytes 491528 | tf_op jit(solution)/shard_map/ppermute | solution.py:338
  31.4 5.5 %collective-permute-start.5 = (bf16[32,3200]{1,0:T(8,128)(2,1)S(1)}, bf16[32,3200]{1,0:T(8,128)(2,1)S(1)}, u32[]{:S(2)}, u32[]{:S(2)}) collective-permute-start(bf16[32,3200]{1,0:T(8,128)(2,1)S(1)} %collective-permute-done.1.refs_1_), channel_id=1, source_target_pairs={{0,1},{1,0},{2,3},{3,2},{16,17},{17,16},{18,19},{19,18},{4,5},{5,4... | collective-permute-start | bytes 614408 | tf_op jit(solution)/shard_map/ppermute | solution.py:338
  31.5 5.3 %collective-permute-start.6 = (bf16[32,3200]{1,0:T(8,128)(2,1)S(1)}, bf16[32,3200]{1,0:T(8,128)(2,1)S(1)}, u32[]{:S(2)}, u32[]{:S(2)}) collective-permute-start(bf16[32,3200]{1,0:T(8,128)(2,1)S(1)} %collective-permute-done.2.refs_2_), channel_id=1, source_target_pairs={{0,1},{1,0},{2,3},{3,2},{16,17},{17,16},{18,19},{19,18},{4,5},{5,4... | collective-permute-start | bytes 614408 | tf_op jit(solution)/shard_map/ppermute | solution.py:338
  31.9 5.0 %collective-permute-start.7 = (bf16[32,3200]{1,0:T(8,128)(2,1)S(1)}, bf16[32,3200]{1,0:T(8,128)(2,1)S(1)}, u32[]{:S(2)}, u32[]{:S(2)}) collective-permute-start(bf16[32,3200]{1,0:T(8,128)(2,1)S(1)} %collective-permute-done.3.refs_3_), channel_id=1, source_target_pairs={{0,1},{1,0},{2,3},{3,2},{16,17},{17,16},{18,19},{19,18},{4,5},{5,4... | collective-permute-start | bytes 614408 | tf_op jit(solution)/shard_map/ppermute | solution.py:338
  46.4 2.6 %collective-permute-start.13 = (bf16[960,512]{1,0:T(8,128)(2,1)S(1)}, bf16[960,512]{1,0:T(8,128)(2,1)S(1)}, u32[]{:S(2)}, u32[]{:S(2)}) collective-permute-start(bf16[960,512]{1,0:T(8,128)(2,1)S(1)} %get-tuple-element.59), channel_id=1, source_target_pairs={{0,1},{1,0},{2,3},{3,2},{16,17},{17,16},{18,19},{19,18},{4,5},{5,4... | collective-permute-start | bytes 2949128 | tf_op jit(solution)/shard_map/ppermute | solution.py:338
  56.1 13.2 %collective-permute-start.14 = (bf16[640,512]{1,0:T(8,128)(2,1)S(1)}, bf16[640,512]{1,0:T(8,128)(2,1)S(1)}, u32[]{:S(2)}, u32[]{:S(2)}) collective-permute-start(bf16[640,512]{1,0:T(8,128)(2,1)S(1)} %get-tuple-element.67), channel_id=1, source_target_pairs={{0,1},{1,0},{2,3},{3,2},{16,17},{17,16},{18,19},{19,18},{4,5},{5,4... | collective-permute-start | bytes 1966088 | tf_op jit(solution)/shard_map/ppermute | solution.py:338
  65.8 8.9 %collective-permute-start.15 = (bf16[960,128]{1,0:T(8,128)(2,1)S(1)}, bf16[960,128]{1,0:T(8,128)(2,1)S(1)}, u32[]{:S(2)}, u32[]{:S(2)}) collective-permute-start(bf16[960,128]{1,0:T(8,128)(2,1)S(1)} %get-tuple-element.75), channel_id=1, source_target_pairs={{0,2},{1,3},{2,0},{3,1},{16,18},{17,19},{18,16},{19,17},{4,6},{5,7... | collective-permute-start | bytes 737288 | tf_op jit(solution)/shard_map/ppermute | solution.py:338
  66.9 14.1 %collective-permute-start.16 = (bf16[960,128]{1,0:T(8,128)(2,1)S(1)}, bf16[960,128]{1,0:T(8,128)(2,1)S(1)}, u32[]{:S(2)}, u32[]{:S(2)}) collective-permute-start(bf16[960,128]{1,0:T(8,128)(2,1)S(1)} %get-tuple-element.76), channel_id=1, source_target_pairs={{0,16},{1,17},{2,18},{3,19},{16,0},{17,1},{18,2},{19,3},{4,20},{5,... | collective-permute-start | bytes 737288 | tf_op jit(solution)/shard_map/ppermute | solution.py:338
  68.4 12.6 %collective-permute-start.17 = (bf16[960,128]{1,0:T(8,128)(2,1)S(1)}, bf16[960,128]{1,0:T(8,128)(2,1)S(1)}, u32[]{:S(2)}, u32[]{:S(2)}) collective-permute-start(bf16[960,128]{1,0:T(8,128)(2,1)S(1)} %get-tuple-element.77), channel_id=1, source_target_pairs={{0,18},{1,19},{2,16},{3,17},{16,2},{17,3},{18,0},{19,1},{4,22},{5,... | collective-permute-start | bytes 737288 | tf_op jit(solution)/shard_map/ppermute | solution.py:338
  69.5 14.0 %collective-permute-start.18 = (bf16[640,128]{1,0:T(8,128)(2,1)S(1)}, bf16[640,128]{1,0:T(8,128)(2,1)S(1)}, u32[]{:S(2)}, u32[]{:S(2)}) collective-permute-start(bf16[640,128]{1,0:T(8,128)(2,1)S(1)} %get-tuple-element.79), channel_id=1, source_target_pairs={{0,2},{1,3},{2,0},{3,1},{16,18},{17,19},{18,16},{19,17},{4,6},{5,7... | collective-permute-start | bytes 491528 | tf_op jit(solution)/shard_map/ppermute | solution.py:338
  70.6 16.6 %collective-permute-start.19 = (bf16[640,128]{1,0:T(8,128)(2,1)S(1)}, bf16[640,128]{1,0:T(8,128)(2,1)S(1)}, u32[]{:S(2)}, u32[]{:S(2)}) collective-permute-start(bf16[640,128]{1,0:T(8,128)(2,1)S(1)} %get-tuple-element.80), channel_id=1, source_target_pairs={{0,16},{1,17},{2,18},{3,19},{16,0},{17,1},{18,2},{19,3},{4,20},{5,... | collective-permute-start | bytes 491528 | tf_op jit(solution)/shard_map/ppermute | solution.py:338
  74.7 12.4 %collective-permute-start.20 = (bf16[640,128]{1,0:T(8,128)(2,1)S(1)}, bf16[640,128]{1,0:T(8,128)(2,1)S(1)}, u32[]{:S(2)}, u32[]{:S(2)}) collective-permute-start(bf16[640,128]{1,0:T(8,128)(2,1)S(1)} %get-tuple-element.81), channel_id=1, source_target_pairs={{0,18},{1,19},{2,16},{3,17},{16,2},{17,3},{18,0},{19,1},{4,22},{5,... | collective-permute-start | bytes 491528 | tf_op jit(solution)/shard_map/ppermute | solution.py:338
  81.2 6.2 %collective-permute-start.21 = (bf16[960,128]{1,0:T(8,128)(2,1)S(1)}, bf16[960,128]{1,0:T(8,128)(2,1)S(1)}, u32[]{:S(2)}, u32[]{:S(2)}) collective-permute-start(bf16[960,128]{1,0:T(8,128)(2,1)S(1)} %fusion.refs_0_), channel_id=1, source_target_pairs={{0,1},{1,0},{2,3},{3,2},{16,17},{17,16},{18,19},{19,18},{4,5},{5,4... | collective-permute-start | bytes 737288 | tf_op jit(solution)/shard_map/ppermute | solution.py:338
  93.6 7.1 %collective-permute-start.24 = (bf16[128,640]{1,0:T(8,128)(2,1)S(1)}, bf16[128,640]{1,0:T(8,128)(2,1)S(1)}, u32[]{:S(2)}, u32[]{:S(2)}) collective-permute-start(bf16[128,640]{1,0:T(8,128)(2,1)S(1)} %get-tuple-element.85), channel_id=1, source_target_pairs={{0,4},{4,0},{8,12},{12,8},{1,5},{5,1},{9,13},{13,9},{2,6},{6,2},{1... | collective-permute-start | bytes 491528 | tf_op jit(solution)/shard_map/ppermute | solution.py:344
  94.4 9.2 %collective-permute-start.23 = (bf16[128,640]{1,0:T(8,128)(2,1)S(1)}, bf16[128,640]{1,0:T(8,128)(2,1)S(1)}, u32[]{:S(2)}, u32[]{:S(2)}) collective-permute-start(bf16[128,640]{1,0:T(8,128)(2,1)S(1)} %get-tuple-element.83), channel_id=1, source_target_pairs={{0,4},{4,0},{8,12},{12,8},{1,5},{5,1},{9,13},{13,9},{2,6},{6,2},{1... | collective-permute-start | bytes 491528 | tf_op jit(solution)/shard_map/ppermute | solution.py:344
  100.8 10.1 %collective-permute-start.25 = (bf16[128,640]{1,0:T(8,128)(2,1)S(1)}, bf16[128,640]{1,0:T(8,128)(2,1)S(1)}, u32[]{:S(2)}, u32[]{:S(2)}) collective-permute-start(bf16[128,640]{1,0:T(8,128)(2,1)S(1)} %add_convert_fusion.3), channel_id=1, source_target_pairs={{0,8},{4,12},{8,0},{12,4},{1,9},{5,13},{9,1},{13,5},{2,10},{6,14},... | collective-permute-start | bytes 491528 | tf_op jit(solution)/shard_map/ppermute | solution.py:344
  (9 other events, 55.7 us)
